TPU v7x, 256 devices: a whole 4x4x8 slice. The times are simulated.
256 devices in a mesh: row: 32 (over z_lo, y, core), col: 8 (over x, z_hi).
Axes of the slice: x: 4, y: 4, z: 8 (z_hi: 2, z_lo: 4; z = z_hi * 4 + z_lo), core: 2. Of those that a mesh axis runs over, the one named last changes fastest.
Arguments:
- object_field: float32 [2, 8192, 2048], P(None, 'row', 'col'), may hold values from -6 to 6
- probe_field: float32 [2, 256, 256], replicated, may hold values from -6 to 6
- intensity: float32 [32, 8, 4, 256, 256], P('row', 'col'), may hold values from 0.25 to 16
- view_offsets: int32 [32, 8, 4, 2], P('row', 'col'), may hold values from 0 to 128
- view_counts: int32 [32, 8], P('row', 'col'), may hold values from 1 to 4, as said below
Outputs:
- updated_object: float32 [2, 8192, 2048], P(None, 'row', 'col')
Inputs may be any that keep to these rules, and one draw needn't show every extreme that they name: `view_counts`: every draw has some tile with 4 valid views. `view_offsets`: each view lies inside its tile's padded window.
All inputs are finite; a program needn't handle non-finite values.
Results may differ from a plain program's by a relative error of at most 0.0003.
Values sent between devices are 32-bit elements; how exact they have to be, the bound alone decides.
A program may use at most 64 MiB of HBM per device.

v0:
```python
import functools

import jax
import jax.numpy as jnp
import ml_dtypes
import numpy as np
from jax import lax
from jax.experimental import pallas as pl
from jax.experimental.pallas import tpu as pltpu
from jax.sharding import PartitionSpec as P

MESH = pl.DeviceIdType.MESH
CORE = 256
MARGIN = 64
HALF = 128
smooth_eps = 0.1
step_size = 0.2
f32, bf16 = jnp.float32, jnp.bfloat16


def dft_tables():
    index = np.arange(HALF)
    forms = []
    for parity in (0, 1):
        turns = (index[:, None] * (2 * index[None, :] + parity)) % CORE
        entries = np.exp(-2j * np.pi * turns / CORE) / np.sqrt(CORE)
        forms.append(np.block([[entries.real, entries.imag], [-entries.imag, entries.real]]))
    forms = np.stack(forms).astype(np.float32)
    forms = np.stack([forms, np.swapaxes(forms, 1, 2)])
    high = forms.astype(ml_dtypes.bfloat16)
    low = (forms - high.astype(np.float32)).astype(ml_dtypes.bfloat16)
    return np.stack([high, low], axis=2)


def order_tables():
    move = np.zeros((CORE, CORE), np.float32)
    index = np.arange(HALF)
    move[2 * index, index] = 1.0
    move[2 * index + 1, HALF + index] = 1.0
    return np.stack([move, move.T]).astype(ml_dtypes.bfloat16)


def dot(left, right):
    return jnp.dot(left, right, preferred_element_type=f32)


def split(value):
    high = value.astype(bf16)
    return high, (value - high.astype(f32)).astype(bf16)


def times_table(value, tab, form, parity):
    high, low = split(value)
    t_high, t_low = tab[form, parity, 0], tab[form, parity, 1]
    return dot(high, t_high) + dot(low, t_high) + dot(high, t_low)


def table_times(value, tab, form, parity):
    high, low = split(value)
    t_high, t_low = tab[form, parity, 0], tab[form, parity, 1]
    return dot(t_high, high) + dot(t_high, low) + dot(t_low, high)


def lanes(*parts):
    return jnp.concatenate(parts, axis=1)


def rows(*parts):
    return jnp.concatenate(parts, axis=0)


def columns(tile):
    return slice(HALF * tile, HALF * tile + HALF)


def prepare_intensity(measured, order, scaled, number):
    right, left = order[0], order[1]
    value = measured[number]
    first = value.astype(bf16)
    rest = value - first.astype(f32)
    second = rest.astype(bf16)
    third = (rest - second.astype(f32)).astype(bf16)
    moved = [dot(left, dot(part, right).astype(bf16)) for part in (first, second, third)]
    total = (moved[0] + moved[1] + moved[2]) + smooth_eps
    scaled[number, 0] = total[:HALF]
    scaled[number, 1] = total[HALF:]


def prepare_probe(probe, rolled, number, row_off, col_off):
    for part in range(2):
        turned = pltpu.roll(probe[part], lax.rem(row_off + CORE, CORE), 0)
        rolled[number, part] = pltpu.roll(turned, lax.rem(col_off + CORE, CORE), 1)


def one_view(number, row_off, col_off, valid, core, side, ends, corner, rolled, scaled, tab, sums):
    lane = lax.broadcasted_iota(jnp.int32, (1, HALF), 1)
    line = lax.broadcasted_iota(jnp.int32, (MARGIN, 1), 0)
    in_side = (lane < col_off, lane >= HALF + col_off)
    in_low, in_high = line < row_off, line >= MARGIN + row_off

    def patch(part, tile):
        middle = jnp.where(in_side[tile], side[part], core[part, :, columns(tile)])
        outer = jnp.where(in_side[tile], corner[part], ends[part, :, columns(tile)])
        low = jnp.where(in_low, outer[:64], middle[:64])
        high = jnp.where(in_high, outer[64:], middle[192:])
        return rows(low, middle[64:192], high)

    waves = []
    for tile in range(2):
        p_re, p_im = rolled[number, 0, :, columns(tile)], rolled[number, 1, :, columns(tile)]
        o_re, o_im = patch(0, tile), patch(1, tile)
        waves.append(lanes(p_re * o_re - p_im * o_im, p_re * o_im + p_im * o_re))
    even = times_table(waves[0] + waves[1], tab, 0, 0)
    odd = times_table(waves[0] - waves[1], tab, 0, 1)

    def stacked(even_cols, odd_cols):
        return rows(
            lanes(even_cols[:, :HALF], odd_cols[:, :HALF]),
            lanes(even_cols[:, HALF:], odd_cols[:, HALF:]),
        )

    halves = (
        stacked(even[:HALF] + even[HALF:], odd[:HALF] + odd[HALF:]),
        stacked(even[:HALF] - even[HALF:], odd[:HALF] - odd[HALF:]),
    )
    back = []
    for parity in range(2):
        far = table_times(halves[parity], tab, 1, parity)
        far_re, far_im = far[:HALF], far[HALF:]
        wanted = scaled[number, parity]
        found = far_re * far_re + far_im * far_im + smooth_eps
        scaling = 1.0 - wanted * lax.rsqrt(wanted * found)
        corrected = rows(far_re * scaling, far_im * scaling)
        back.append(table_times(corrected, tab, 0, parity))
    upper, lower = back[0] + back[1], back[0] - back[1]
    re = rows(upper[:HALF], lower[:HALF])
    im = rows(upper[HALF:], lower[HALF:])
    even = times_table(lanes(re[:, :HALF], im[:, :HALF]), tab, 1, 0)
    odd = times_table(lanes(re[:, HALF:], im[:, HALF:]), tab, 1, 1)
    core_sum, side_sum, ends_sum, corner_sum = sums
    for tile, wave in ((0, even + odd), (1, even - odd)):
        b_re, b_im = wave[:, :HALF], wave[:, HALF:]
        p_re, p_im = rolled[number, 0, :, columns(tile)], rolled[number, 1, :, columns(tile)]
        for part, raw in ((0, p_re * b_re + p_im * b_im), (1, p_re * b_im - p_im * b_re)):
            grad = raw * valid
            outside = jnp.where(in_side[tile], grad, 0.0)
            inside = jnp.where(in_side[tile], 0.0, grad)
            for value, main, edge, where in (
                (inside, core_sum, ends_sum, columns(tile)),
                (outside, side_sum, corner_sum, slice(0, HALF)),
            ):
                low = jnp.where(in_low, value[:64], 0.0)
                high = jnp.where(in_high, value[192:], 0.0)
                kept = rows(value[:64] - low, value[64:192], value[192:] - high)
                main[part, :, where] = main[part, :, where] + kept
                edge[part, :, where] = edge[part, :, where] + rows(low, high)


CHUNKS = ((0, 64), (192, 64), (64, 128))


def step_kernel(
    n_row, n_col,
    object_hbm, probe_hbm, intensity_hbm, offsets_hbm, counts_hbm, tab_hbm, order_hbm,
    out_ref,
    core, probe, measured, tab, order, offsets, counts,
    pack, got, ends, corner_got, side, corner, rolled, scaled,
    core_sum, side_sum, ends_sum, corner_sum,
    back_pack, back_got, back_ends, back_corner,
    load_sem, send_sem, recv_sem,
):
    r, c = lax.axis_index("row"), lax.axis_index("col")
    has = {"left": c > 0, "right": c < n_col - 1, "up": r > 0, "down": r < n_row - 1}
    where = {"left": (r, c - 1), "right": (r, c + 1), "up": (r - 1, c), "down": (r + 1, c)}
    opposite = {"left": "right", "right": "left", "up": "down", "down": "up"}

    barrier = pltpu.get_barrier_semaphore()
    for way in where:
        @pl.when(has[way])
        def _():
            pl.semaphore_signal(barrier, inc=1, device_id=where[way], device_id_type=MESH)

    loads = [
        pltpu.make_async_copy(source, target, load_sem.at[at])
        for at, (source, target) in enumerate((
            (object_hbm, core), (offsets_hbm, offsets), (counts_hbm, counts), (probe_hbm, probe),
            (intensity_hbm, measured), (order_hbm, order), (tab_hbm, tab),
        ))
    ]
    for load in loads:
        load.start()

    def copy(at, way, source, target):
        return pltpu.make_async_remote_copy(
            src_ref=source, dst_ref=target, send_sem=send_sem.at[at], recv_sem=recv_sem.at[at],
            device_id=where[way], device_id_type=MESH,
        )

    sent = []

    def send(at, way, source, target):
        made = copy(at, way, source, target)
        sent.append((way, made))

        @pl.when(has[way])
        def _():
            made.start()

        return made

    def receive(way, made):
        @pl.when(has[opposite[way]])
        def _():
            made.wait_recv()

    zeros = jnp.zeros
    for way, spots in {
        "right": ((got, 0), (back_got, 1)),
        "left": ((got, 1), (back_got, 0)),
    }.items():
        @pl.when(jnp.logical_not(has[way]))
        def _():
            for ref, at in spots:
                ref[at] = zeros(ref.shape[1:], f32)
    for way, at in (("down", 0), ("up", 64)):
        @pl.when(jnp.logical_not(has[way]))
        def _():
            for ref in (ends, corner_got):
                ref[:, at : at + 64, :] = zeros((2, 64, ref.shape[2]), f32)
    for way, at in (("up", 0), ("down", 64)):
        @pl.when(jnp.logical_not(has[way]))
        def _():
            for ref in (back_ends, back_corner):
                ref[:, at : at + 64, :] = zeros((2, 64, ref.shape[2]), f32)
    for ref in (core_sum, side_sum, ends_sum, corner_sum):
        ref[...] = jnp.zeros_like(ref)

    first_half = lax.broadcasted_iota(jnp.int32, (1, HALF), 1) < MARGIN

    def turned(value):
        return pltpu.roll(value, MARGIN, 1)

    loads[0].wait()
    pack[0] = jnp.where(first_half, core[0, :, :HALF], turned(core[1, :, :HALF]))
    pack[1] = jnp.where(first_half, turned(core[0, :, HALF:]), core[1, :, HALF:])

    peers = sum(jnp.where(has[way], 1, 0) for way in where)
    pl.semaphore_wait(barrier, peers)

    at = 0
    fore = {}
    for start, size in CHUNKS:
        for slot, way in ((0, "left"), (1, "right")):
            part = pl.ds(start, size)
            fore[start, way] = send(at, way, pack.at[slot, part], got.at[slot, part])
            at += 1
    ends_up = send(at, "up", core.at[:, pl.ds(0, 64)], ends.at[:, pl.ds(0, 64)])
    ends_down = send(at + 1, "down", core.at[:, pl.ds(192, 64)], ends.at[:, pl.ds(64, 64)])
    at += 2

    for load in loads[1:]:
        load.wait()
    for number in range(4):
        prepare_probe(probe, rolled, number, offsets[0, number] - MARGIN, offsets[1, number] - MARGIN)
    for number in range(4):
        prepare_intensity(measured, order, scaled, number)

    for way in ("left", "right"):
        receive(way, fore[0, way])
    corner_up = send(at, "up", got.at[:, pl.ds(0, 64)], corner_got.at[:, pl.ds(0, 64)])
    for way in ("left", "right"):
        receive(way, fore[192, way])
    corner_down = send(at + 1, "down", got.at[:, pl.ds(192, 64)], corner_got.at[:, pl.ds(64, 64)])
    at += 2
    for way in ("left", "right"):
        receive(way, fore[64, way])
    side[0] = jnp.where(first_half, got[0], turned(got[1]))
    side[1] = jnp.where(first_half, turned(got[0]), got[1])
    receive("up", ends_up)
    receive("down", ends_down)
    receive("up", corner_up)
    receive("down", corner_down)
    corner[0] = jnp.where(first_half, corner_got[0], turned(corner_got[1]))
    corner[1] = jnp.where(first_half, turned(corner_got[0]), corner_got[1])

    @pl.loop(0, 4)
    def _(number):
        valid = jnp.where(number < counts[0, 0], 1.0, 0.0)
        one_view(
            number, offsets[0, number] - MARGIN, offsets[1, number] - MARGIN, valid, core, side, ends, corner,
            rolled, scaled, tab, (core_sum, side_sum, ends_sum, corner_sum),
        )

    grads = []
    for way, start in (("down", 0), ("up", 64)):
        part = pl.ds(start, 64)
        grads.append((way, start, send(at, way, corner_sum.at[:, part], back_corner.at[:, part])))
        at += 1
    back = {}

    def pack_sides(start, size):
        part = slice(start, start + size)
        re, im = side_sum[0, part], side_sum[1, part]
        back_pack[0, part] = jnp.where(first_half, re, turned(im))
        back_pack[1, part] = jnp.where(first_half, turned(re), im)

    def send_sides(start, size):
        nonlocal at
        part = pl.ds(start, size)
        for slot, way in ((0, "right"), (1, "left")):
            back[start, way] = send(at, way, back_pack.at[slot, part], back_got.at[slot, part])
            at += 1

    pack_sides(64, 128)
    send_sides(64, 128)
    edge = []
    for way, start in (("down", 0), ("up", 64)):
        part = pl.ds(start, 64)
        edge.append((way, start, send(at, way, ends_sum.at[:, part], back_ends.at[:, part])))
        at += 1
    for way, start, made in grads:
        receive(way, made)
        begin = 0 if start == 0 else 192
        side_sum[:, begin : begin + 64] = side_sum[:, begin : begin + 64] + back_corner[:, start : start + 64]
        pack_sides(begin, 64)
        send_sides(begin, 64)
    for way, start, made in edge:
        receive(way, made)
        begin = 0 if start == 0 else 192
        core_sum[:, begin : begin + 64] = core_sum[:, begin : begin + 64] + back_ends[:, start : start + 64]
    out_ref[...] = core[...] - step_size * core_sum[...]
    for start, size in ((64, 128), (0, 64), (192, 64)):
        part = slice(start, start + size)
        for way in ("right", "left"):
            receive(way, back[start, way])
        from_left, from_right = back_got[0, part], back_got[1, part]
        for at_part, left_part, right_part in (
            (0, from_left, turned(from_right)),
            (1, turned(from_left), from_right),
        ):
            out_ref[at_part, part, :HALF] = out_ref[at_part, part, :HALF] - step_size * jnp.where(first_half, left_part, 0.0)
            out_ref[at_part, part, HALF:] = out_ref[at_part, part, HALF:] - step_size * jnp.where(first_half, 0.0, right_part)
    for way, made in sent:
        @pl.when(has[way])
        def _():
            made.wait_send()


def per_device(n_row, n_col, object_field, probe_field, intensity, view_offsets, view_counts):
    anywhere = pl.BlockSpec(memory_space=pl.ANY)
    vmem = pltpu.VMEM
    n_copies = 20
    return pl.pallas_call(
        functools.partial(step_kernel, n_row, n_col),
        out_shape=jax.ShapeDtypeStruct(object_field.shape, f32),
        in_specs=[anywhere] * 7,
        out_specs=pl.BlockSpec(memory_space=vmem),
        scratch_shapes=[
            vmem((2, 256, 256), f32), vmem((2, 256, 256), f32), vmem((4, 256, 256), f32),
            vmem((2, 2, 2, 256, 256), bf16), vmem((2, 256, 256), bf16),
            pltpu.SMEM((2, 4), jnp.int32), pltpu.SMEM((1, 1), jnp.int32),
            vmem((2, 256, 128), f32), vmem((2, 256, 128), f32), vmem((2, 128, 256), f32), vmem((2, 128, 128), f32),
            vmem((2, 256, 128), f32), vmem((2, 128, 128), f32),
            vmem((4, 2, 256, 256), f32), vmem((4, 2, 128, 256), f32),
            vmem((2, 256, 256), f32), vmem((2, 256, 128), f32), vmem((2, 128, 256), f32), vmem((2, 128, 128), f32),
            vmem((2, 256, 128), f32), vmem((2, 256, 128), f32), vmem((2, 128, 256), f32), vmem((2, 128, 128), f32),
            pltpu.SemaphoreType.DMA((7,)), pltpu.SemaphoreType.DMA((n_copies,)), pltpu.SemaphoreType.DMA((n_copies,)),
        ],
        compiler_params=pltpu.CompilerParams(
            collective_id=0, has_side_effects=True, vmem_limit_bytes=56 * 2**20
        ),
    )(
        object_field, probe_field, intensity[0, 0], view_offsets[0, 0].T, view_counts,
        jnp.asarray(dft_tables()), jnp.asarray(order_tables()),
    )


def solution(mesh):
    in_specs = (
        P(None, "row", "col"),
        P(),
        P("row", "col", None, None, None),
        P("row", "col", None, None),
        P("row", "col"),
    )
    out_specs = P(None, "row", "col")
    body = functools.partial(per_device, mesh.shape["row"], mesh.shape["col"])
    return jax.shard_map(body, mesh=mesh, in_specs=in_specs, out_specs=out_specs, check_vma=False)
```

profile of v0, /device:TPU:27, one launch (start us, length us, event | category | flops | bytes accessed | tf_op | source)
XLA Modules:
  0.0 48.5 jit_solution(14580469044476743204)
XLA Ops:
  0.7 46.0 %shard_map.73 = f32[2,256,256]{2,1,0:T(8,128)} custom-call(f32[2,256,256]{2,1,0:T(8,128)} %object_hbm.1, f32[2,256,256]{2,1,0:T(8,128)} %probe_hbm.1, f32[4,256,256]{2,1,0:T(8,128)} %bitcast.4, s32[2,4]{1,0:T(2,128)} %bitcast.5, s32[1,1]{1,0:T(1,128)S(6)} %copy.9.counts_hbm, bf16[2,2,2,256,256]{4,3,2,1,0:T(8,128)(2,1)} %constant.4.clone.tab_hbm, ...), custom_call_target="tpu_custom_call" | custom-call | tf_op jit(solution)/shard_map/pallas_call | solution.py:353
  46.6 1.9 %copy.10 = f32[2,256,256]{2,1,0:T(8,128)} copy(f32[2,256,256]{2,1,0:T(8,128)} %shard_map.73) | data formatting | bytes 1048576
where the time goes:
time: 48.6 us; the launch traced here: 48.5 us
  Pallas kernels  46 us (95%)
  local copies, waits for them, and re-layouts  1.87 us (4%)
  between operations  0.66 us (1%)
    pallas_call x1, Pallas kernels, per_device(): pl.pallas_call(functools.partial(step_kernel, n_row, n_col), out_shape=ja...  46 us
    unnamed x1, local copies, waits for them, and re-layouts  1.87 us

commit v1 on v0

--- a/solution.py
+++ b/solution.py
@@ -29,7 +29,7 @@
     forms = np.stack([forms, np.swapaxes(forms, 1, 2)])
     high = forms.astype(ml_dtypes.bfloat16)
     low = (forms - high.astype(np.float32)).astype(ml_dtypes.bfloat16)
-    return np.stack([high, low], axis=2)
+    return np.stack([high, low], axis=2).reshape(8, CORE, CORE)
 
 
 def order_tables():
@@ -40,6 +40,10 @@
     return np.stack([move, move.T]).astype(ml_dtypes.bfloat16)
 
 
+def table(tab, form, parity, low):
+    return tab[4 * form + 2 * parity + low]
+
+
 def dot(left, right):
     return jnp.dot(left, right, preferred_element_type=f32)
 
@@ -51,13 +55,13 @@
 
 def times_table(value, tab, form, parity):
     high, low = split(value)
-    t_high, t_low = tab[form, parity, 0], tab[form, parity, 1]
+    t_high, t_low = table(tab, form, parity, 0), table(tab, form, parity, 1)
     return dot(high, t_high) + dot(low, t_high) + dot(high, t_low)
 
 
 def table_times(value, tab, form, parity):
     high, low = split(value)
-    t_high, t_low = tab[form, parity, 0], tab[form, parity, 1]
+    t_high, t_low = table(tab, form, parity, 0), table(tab, form, parity, 1)
     return dot(t_high, high) + dot(t_high, low) + dot(t_low, high)
 
 
@@ -73,8 +77,8 @@
     return slice(HALF * tile, HALF * tile + HALF)
 
 
-def prepare_intensity(measured, order, scaled, number):
-    right, left = order[0], order[1]
+def prepare_intensity(measured, tab, scaled, number):
+    right, left = tab[8], tab[9]
     value = measured[number]
     first = value.astype(bf16)
     rest = value - first.astype(f32)
@@ -110,8 +114,10 @@
         p_re, p_im = rolled[number, 0, :, columns(tile)], rolled[number, 1, :, columns(tile)]
         o_re, o_im = patch(0, tile), patch(1, tile)
         waves.append(lanes(p_re * o_re - p_im * o_im, p_re * o_im + p_im * o_re))
+    yield
     even = times_table(waves[0] + waves[1], tab, 0, 0)
     odd = times_table(waves[0] - waves[1], tab, 0, 1)
+    yield
 
     def stacked(even_cols, odd_cols):
         return rows(
@@ -123,20 +129,23 @@
         stacked(even[:HALF] + even[HALF:], odd[:HALF] + odd[HALF:]),
         stacked(even[:HALF] - even[HALF:], odd[:HALF] - odd[HALF:]),
     )
+    fars = [table_times(halves[parity], tab, 1, parity) for parity in range(2)]
+    yield
     back = []
-    for parity in range(2):
-        far = table_times(halves[parity], tab, 1, parity)
+    for parity, far in enumerate(fars):
         far_re, far_im = far[:HALF], far[HALF:]
         wanted = scaled[number, parity]
         found = far_re * far_re + far_im * far_im + smooth_eps
         scaling = 1.0 - wanted * lax.rsqrt(wanted * found)
         corrected = rows(far_re * scaling, far_im * scaling)
         back.append(table_times(corrected, tab, 0, parity))
+    yield
     upper, lower = back[0] + back[1], back[0] - back[1]
     re = rows(upper[:HALF], lower[:HALF])
     im = rows(upper[HALF:], lower[HALF:])
     even = times_table(lanes(re[:, :HALF], im[:, :HALF]), tab, 1, 0)
     odd = times_table(lanes(re[:, HALF:], im[:, HALF:]), tab, 1, 1)
+    yield
     core_sum, side_sum, ends_sum, corner_sum = sums
     for tile, wave in ((0, even + odd), (1, even - odd)):
         b_re, b_im = wave[:, :HALF], wave[:, HALF:]
@@ -144,16 +153,18 @@
         for part, raw in ((0, p_re * b_re + p_im * b_im), (1, p_re * b_im - p_im * b_re)):
             grad = raw * valid
             outside = jnp.where(in_side[tile], grad, 0.0)
-            inside = jnp.where(in_side[tile], 0.0, grad)
             for value, main, edge, where in (
-                (inside, core_sum, ends_sum, columns(tile)),
+                (grad - outside, core_sum, ends_sum, columns(tile)),
                 (outside, side_sum, corner_sum, slice(0, HALF)),
             ):
                 low = jnp.where(in_low, value[:64], 0.0)
                 high = jnp.where(in_high, value[192:], 0.0)
-                kept = rows(value[:64] - low, value[64:192], value[192:] - high)
-                main[part, :, where] = main[part, :, where] + kept
-                edge[part, :, where] = edge[part, :, where] + rows(low, high)
+                main[part, :64, where] = main[part, :64, where] + (value[:64] - low)
+                main[part, 64:192, where] = main[part, 64:192, where] + value[64:192]
+                main[part, 192:, where] = main[part, 192:, where] + (value[192:] - high)
+                edge[part, :64, where] = edge[part, :64, where] + low
+                edge[part, 64:, where] = edge[part, 64:, where] + high
+    yield
 
 
 CHUNKS = ((0, 64), (192, 64), (64, 128))
@@ -161,9 +172,9 @@
 
 def step_kernel(
     n_row, n_col,
-    object_hbm, probe_hbm, intensity_hbm, offsets_hbm, counts_hbm, tab_hbm, order_hbm,
+    object_hbm, probe_hbm, intensity_hbm, offsets_hbm, counts_hbm, tab_hbm,
     out_ref,
-    core, probe, measured, tab, order, offsets, counts,
+    core, probe, measured, tab, offsets, counts,
     pack, got, ends, corner_got, side, corner, rolled, scaled,
     core_sum, side_sum, ends_sum, corner_sum,
     back_pack, back_got, back_ends, back_corner,
@@ -184,7 +195,7 @@
         pltpu.make_async_copy(source, target, load_sem.at[at])
         for at, (source, target) in enumerate((
             (object_hbm, core), (offsets_hbm, offsets), (counts_hbm, counts), (probe_hbm, probe),
-            (intensity_hbm, measured), (order_hbm, order), (tab_hbm, tab),
+            (intensity_hbm, measured), (tab_hbm, tab),
         ))
     ]
     for load in loads:
@@ -263,7 +274,7 @@
     for number in range(4):
         prepare_probe(probe, rolled, number, offsets[0, number] - MARGIN, offsets[1, number] - MARGIN)
     for number in range(4):
-        prepare_intensity(measured, order, scaled, number)
+        prepare_intensity(measured, tab, scaled, number)
 
     for way in ("left", "right"):
         receive(way, fore[0, way])
@@ -283,13 +294,17 @@
     corner[0] = jnp.where(first_half, corner_got[0], turned(corner_got[1]))
     corner[1] = jnp.where(first_half, turned(corner_got[0]), corner_got[1])
 
-    @pl.loop(0, 4)
-    def _(number):
+    def view(number):
         valid = jnp.where(number < counts[0, 0], 1.0, 0.0)
-        one_view(
+        return one_view(
             number, offsets[0, number] - MARGIN, offsets[1, number] - MARGIN, valid, core, side, ends, corner,
             rolled, scaled, tab, (core_sum, side_sum, ends_sum, corner_sum),
         )
+
+    @pl.loop(0, 2)
+    def _(pair):
+        for _ in zip(view(2 * pair), view(2 * pair + 1)):
+            pass
 
     grads = []
     for way, start in (("down", 0), ("up", 64)):
@@ -353,25 +368,25 @@
     return pl.pallas_call(
         functools.partial(step_kernel, n_row, n_col),
         out_shape=jax.ShapeDtypeStruct(object_field.shape, f32),
-        in_specs=[anywhere] * 7,
+        in_specs=[anywhere] * 6,
         out_specs=pl.BlockSpec(memory_space=vmem),
         scratch_shapes=[
             vmem((2, 256, 256), f32), vmem((2, 256, 256), f32), vmem((4, 256, 256), f32),
-            vmem((2, 2, 2, 256, 256), bf16), vmem((2, 256, 256), bf16),
+            vmem((10, 256, 256), bf16),
             pltpu.SMEM((2, 4), jnp.int32), pltpu.SMEM((1, 1), jnp.int32),
             vmem((2, 256, 128), f32), vmem((2, 256, 128), f32), vmem((2, 128, 256), f32), vmem((2, 128, 128), f32),
             vmem((2, 256, 128), f32), vmem((2, 128, 128), f32),
             vmem((4, 2, 256, 256), f32), vmem((4, 2, 128, 256), f32),
             vmem((2, 256, 256), f32), vmem((2, 256, 128), f32), vmem((2, 128, 256), f32), vmem((2, 128, 128), f32),
             vmem((2, 256, 128), f32), vmem((2, 256, 128), f32), vmem((2, 128, 256), f32), vmem((2, 128, 128), f32),
-            pltpu.SemaphoreType.DMA((7,)), pltpu.SemaphoreType.DMA((n_copies,)), pltpu.SemaphoreType.DMA((n_copies,)),
+            pltpu.SemaphoreType.DMA((6,)), pltpu.SemaphoreType.DMA((n_copies,)), pltpu.SemaphoreType.DMA((n_copies,)),
         ],
         compiler_params=pltpu.CompilerParams(
-            collective_id=0, has_side_effects=True, vmem_limit_bytes=56 * 2**20
+            collective_id=0, has_side_effects=True, vmem_limit_bytes=55574528
         ),
     )(
         object_field, probe_field, intensity[0, 0], view_offsets[0, 0].T, view_counts,
-        jnp.asarray(dft_tables()), jnp.asarray(order_tables()),
+        jnp.asarray(np.concatenate([dft_tables(), order_tables()])),
     )
 
 

time: 48.6 us -> 44.2 us (0.909)
  Pallas kernels: 46 us -> 42 us
    pallas_call x1, Pallas kernels: 46 us -> 42 us  [per_device(): pl.pallas_call(functools.partial(step_kernel, n_row, n_col), out_shape=ja...]
    unnamed x1 -> x3, local copies, waits for them, and re-layouts: 1.87 us -> 1.47 us
where the time goes in v1:
time: 44.2 us; the launch traced here: 44.1 us
  Pallas kernels  42 us (95%)
  local copies, waits for them, and re-layouts  1.47 us (3%)
  between operations  0.67 us (2%)
    pallas_call x1, Pallas kernels, per_device(): pl.pallas_call(functools.partial(step_kernel, n_row, n_col), out_shape=ja...  42 us
    unnamed x3, local copies, waits for them, and re-layouts  1.47 us

profile of v1, /device:TPU:27, one launch (start us, length us, event | category | flops | bytes accessed | tf_op | source)
XLA Modules:
  0.0 44.1 jit_solution(16553792926630213768)
XLA Ops:
  0.7 0.0 copy-start
  0.7 0.7 %copy-done = s32[1,1,4,2]{2,3,1,0:T(2,128)S(1)} copy-done((s32[1,1,4,2]{2,3,1,0:T(2,128)S(1)}, s32[1,1,4,2]{2,3,1,0:T(2,128)}, u32[]{:S(2)}) %copy-start) | copy-done | bytes 56
  1.3 42.0 %shard_map.64 = f32[2,256,256]{2,1,0:T(8,128)S(1)} custom-call(f32[2,256,256]{2,1,0:T(8,128)} %object_hbm.1, f32[2,256,256]{2,1,0:T(8,128)} %probe_hbm.1, f32[4,256,256]{2,1,0:T(8,128)} %bitcast.5, s32[2,4]{1,0:T(2,128)S(1)} %bitcast.4, s32[1,1]{1,0:T(1,128)S(6)} %copy.8.counts_hbm, bf16[10,256,256]{2,1,0:T(8,128)(2,1)} %constant.2.clone.tab_hbm), custom_call_target="tpu_custom_call" | custom-call | tf_op jit(solution)/shard_map/pallas_call | solution.py:368
  43.3 0.8 %copy.9 = f32[2,256,256]{2,1,0:T(8,128)} copy(f32[2,256,256]{2,1,0:T(8,128)S(1)} %shard_map.64) | data formatting | bytes 1048576
Async XLA Ops:
  0.7 0.7 %copy-start = (s32[1,1,4,2]{2,3,1,0:T(2,128)S(1)}, s32[1,1,4,2]{2,3,1,0:T(2,128)}, u32[]{:S(2)}) copy-start(s32[1,1,4,2]{2,3,1,0:T(2,128)} %param.9) | copy-start | bytes 100

commit v2 on v1

--- a/solution.py
+++ b/solution.py
@@ -385,7 +385,7 @@
             collective_id=0, has_side_effects=True, vmem_limit_bytes=55574528
         ),
     )(
-        object_field, probe_field, intensity[0, 0], view_offsets[0, 0].T, view_counts,
+        object_field, probe_field, intensity[0, 0], pltpu.with_memory_space_constraint(view_offsets[0, 0].T, pltpu.HBM), view_counts,
         jnp.asarray(np.concatenate([dft_tables(), order_tables()])),
     )
 

time: 44.2 us -> 43.6 us (0.986)
  local copies, waits for them, and re-layouts: 1.47 us -> 0.8 us
    unnamed x3 -> x1, local copies, waits for them, and re-layouts: 1.47 us -> 0.8 us
where the time goes in v2:
time: 43.6 us; the launch traced here: 43.5 us
  Pallas kernels  42.1 us (97%)
  local copies, waits for them, and re-layouts  0.8 us (2%)
  between operations  0.66 us (2%)
    pallas_call x1, Pallas kernels, per_device(): pl.pallas_call(functools.partial(step_kernel, n_row, n_col), out_shape=ja...  42.1 us

profile of v2, /device:TPU:27, one launch (start us, length us, event | category | flops | bytes accessed | tf_op | source)
XLA Modules:
  0.0 43.5 jit_solution(15229719603733809399)
XLA Ops:
  0.7 42.1 %shard_map.64 = f32[2,256,256]{2,1,0:T(8,128)S(1)} custom-call(f32[2,256,256]{2,1,0:T(8,128)} %object_hbm.1, f32[2,256,256]{2,1,0:T(8,128)} %probe_hbm.1, f32[4,256,256]{2,1,0:T(8,128)} %bitcast.4, s32[2,4]{1,0:T(2,128)} %bitcast.5, s32[1,1]{1,0:T(1,128)S(6)} %copy.8.counts_hbm, bf16[10,256,256]{2,1,0:T(8,128)(2,1)} %constant.2.clone.tab_hbm), custom_call_target="tpu_custom_call" | custom-call | tf_op jit(solution)/shard_map/pallas_call | solution.py:368
  42.7 0.8 %copy.9 = f32[2,256,256]{2,1,0:T(8,128)} copy(f32[2,256,256]{2,1,0:T(8,128)S(1)} %shard_map.64) | data formatting | bytes 1048576

commit v3 on v2

--- a/solution.py
+++ b/solution.py
@@ -167,6 +167,10 @@
     yield
 
 
+BACK_CHUNKS = (64, 128, 0, 192)
+BACK_VIA = (64, 0, 192)
+RUN = 8
+RELAY_AT = {("down", 0): 5, ("down", 1): 3, ("up", 0): 2, ("up", 1): 4}
 CHUNKS = ((0, 64), (192, 64), (64, 128))
 
 
@@ -178,6 +182,7 @@
     pack, got, ends, corner_got, side, corner, rolled, scaled,
     core_sum, side_sum, ends_sum, corner_sum,
     back_pack, back_got, back_ends, back_corner,
+    hold, back_hold,
     load_sem, send_sem, recv_sem,
 ):
     r, c = lax.axis_index("row"), lax.axis_index("col")
@@ -185,11 +190,43 @@
     where = {"left": (r, c - 1), "right": (r, c + 1), "up": (r - 1, c), "down": (r + 1, c)}
     opposite = {"left": "right", "right": "left", "up": "down", "down": "up"}
 
+    place = lax.rem(r, RUN)
+    over = {"down": (place == RUN - 1) & has["down"], "up": (place == 0) & has["up"]}
+    near = {way: has[way] & jnp.logical_not(over[way]) for way in over}
+    has_run = {"down": r < n_row - RUN, "up": r >= RUN}
+    relays = {key: (place == RELAY_AT[key]) & has_run[key[0]] for key in RELAY_AT}
+    sign = {"down": 1, "up": -1}
+
+    def row_at(offset):
+        return (r + offset, c)
+
+    def from_source(way, part):
+        return -sign[way] * (2 * part + 2)
+
+    def to_target(way, part):
+        return sign[way] * (2 * part + 3)
+
+    even = lax.rem(c, 2) == 0
+    outward = {"left": even, "right": jnp.logical_not(even)}
+    depth = jnp.where(even, c, n_col - 1 - c)
+    beyond = (r, jnp.where(even, c - 2, c + 2))
+    inner = (r, jnp.where(even, c + 2, c - 2))
+    by_way = [(depth >= 2) & (depth <= n_col - 2 - 2 * level) for level in range(3)]
+    passes = [depth <= n_col - 4 - 2 * level for level in range(3)]
+
     barrier = pltpu.get_barrier_semaphore()
+
+    def greet(condition, device):
+        @pl.when(condition)
+        def _():
+            pl.semaphore_signal(barrier, inc=1, device_id=device, device_id_type=MESH)
+
+    greet(passes[0], inner)
     for way in where:
-        @pl.when(has[way])
-        def _():
-            pl.semaphore_signal(barrier, inc=1, device_id=where[way], device_id_type=MESH)
+        greet(has[way], where[way])
+    for way, part in RELAY_AT:
+        greet(relays[way, part], row_at(-from_source(way, part)))
+        greet(over[opposite[way]], row_at(-to_target(way, part)))
 
     loads = [
         pltpu.make_async_copy(source, target, load_sem.at[at])
@@ -201,23 +238,75 @@
     for load in loads:
         load.start()
 
-    def copy(at, way, source, target):
+    def copy(at, device, source, target, arrival=None):
         return pltpu.make_async_remote_copy(
-            src_ref=source, dst_ref=target, send_sem=send_sem.at[at], recv_sem=recv_sem.at[at],
-            device_id=where[way], device_id_type=MESH,
+            src_ref=source, dst_ref=target, send_sem=send_sem.at[at],
+            recv_sem=recv_sem.at[at if arrival is None else arrival], device_id=device, device_id_type=MESH,
         )
 
     sent = []
 
+    def start(condition, made):
+        sent.append((condition, made))
+
+        @pl.when(condition)
+        def _():
+            made.start()
+
+        return made
+
     def send(at, way, source, target):
-        made = copy(at, way, source, target)
-        sent.append((way, made))
-
-        @pl.when(has[way])
-        def _():
-            made.start()
-
-        return made
+        return start(has[way], copy(at, where[way], source, target))
+
+    def send_chunk(at, way, source, target, held, via_at, level):
+        straight = copy(at, where[way], source, target)
+        if level is None:
+            return start(has[way], straight)
+        around = outward[way] & by_way[level]
+        start(has[way] & jnp.logical_not(around), straight)
+        start(around, copy(at, beyond, source, held, via_at + level))
+        return straight
+
+    def pass_chunk(numbers, targets, held, via_at, level):
+        arriving = copy(via_at + 3 + level, inner, held, held, via_at + level)
+
+        @pl.when(passes[level])
+        def _():
+            arriving.wait_recv()
+
+        for way in ("left", "right"):
+            made = copy(via_at + 3 + level, where[opposite[way]], held, targets[way], numbers[way])
+            start(passes[level] & outward[way], made)
+
+    def strip(ref, part, begin):
+        return ref.at[part, pl.ds(begin, 64)]
+
+    def send_ends(at, source, target, hold, begins):
+        for way, (begin, end) in begins.items():
+            for part in range(2):
+                number = at + 2 * (way == "up") + part
+                piece, spot = strip(source, part, begin), strip(target, part, end)
+                start(near[way], copy(number, where[way], piece, spot))
+                start(over[way], copy(number, row_at(from_source(way, part)), piece, hold, at + 4))
+
+    def pass_ends(at, target, hold, begins):
+        for way, part in RELAY_AT:
+            number = at + 2 * (way == "up") + part
+            spot = strip(target, part, begins[way][1])
+            made = copy(at + 5, row_at(to_target(way, part)), hold, spot, number)
+            arriving = copy(at + 5, row_at(to_target(way, part)), hold, hold, at + 4)
+
+            @pl.when(relays[way, part])
+            def _():
+                arriving.wait_recv()
+
+            start(relays[way, part], made)
+
+    def receive_ends(at, way, source, target, begins):
+        begin, end = begins[way]
+        for part in range(2):
+            number = at + 2 * (way == "up") + part
+            receive(way, copy(number, where[way], strip(source, part, begin), strip(target, part, end)))
 
     def receive(way, made):
         @pl.when(has[opposite[way]])
@@ -255,19 +344,21 @@
     pack[0] = jnp.where(first_half, core[0, :, :HALF], turned(core[1, :, :HALF]))
     pack[1] = jnp.where(first_half, turned(core[0, :, HALF:]), core[1, :, HALF:])
 
-    peers = sum(jnp.where(has[way], 1, 0) for way in where)
+    peers = sum(jnp.where(has[way], 1, 0) for way in where) + jnp.where(by_way[0], 1, 0)
+    peers += sum(jnp.where(relays[key], 1, 0) + jnp.where(over[key[0]], 1, 0) for key in RELAY_AT)
     pl.semaphore_wait(barrier, peers)
 
     at = 0
     fore = {}
-    for start, size in CHUNKS:
+    for begin, size in CHUNKS:
         for slot, way in ((0, "left"), (1, "right")):
-            part = pl.ds(start, size)
-            fore[start, way] = send(at, way, pack.at[slot, part], got.at[slot, part])
+            part = pl.ds(begin, size)
+            fore[begin, way] = send(at, way, pack.at[slot, part], got.at[slot, part])
             at += 1
-    ends_up = send(at, "up", core.at[:, pl.ds(0, 64)], ends.at[:, pl.ds(0, 64)])
-    ends_down = send(at + 1, "down", core.at[:, pl.ds(192, 64)], ends.at[:, pl.ds(64, 64)])
-    at += 2
+    ends_at = at
+    ends_begins = {"down": (192, 64), "up": (0, 0)}
+    send_ends(ends_at, core, ends, hold, ends_begins)
+    at += 6
 
     for load in loads[1:]:
         load.wait()
@@ -279,6 +370,7 @@
     for way in ("left", "right"):
         receive(way, fore[0, way])
     corner_up = send(at, "up", got.at[:, pl.ds(0, 64)], corner_got.at[:, pl.ds(0, 64)])
+    pass_ends(ends_at, ends, hold, ends_begins)
     for way in ("left", "right"):
         receive(way, fore[192, way])
     corner_down = send(at + 1, "down", got.at[:, pl.ds(192, 64)], corner_got.at[:, pl.ds(64, 64)])
@@ -287,8 +379,8 @@
         receive(way, fore[64, way])
     side[0] = jnp.where(first_half, got[0], turned(got[1]))
     side[1] = jnp.where(first_half, turned(got[0]), got[1])
-    receive("up", ends_up)
-    receive("down", ends_down)
+    for way in ("down", "up"):
+        receive_ends(ends_at, way, core, ends, ends_begins)
     receive("up", corner_up)
     receive("down", corner_down)
     corner[0] = jnp.where(first_half, corner_got[0], turned(corner_got[1]))
@@ -307,47 +399,59 @@
             pass
 
     grads = []
-    for way, start in (("down", 0), ("up", 64)):
-        part = pl.ds(start, 64)
-        grads.append((way, start, send(at, way, corner_sum.at[:, part], back_corner.at[:, part])))
+    for way, row in (("down", 0), ("up", 64)):
+        part = pl.ds(row, 64)
+        grads.append((way, row, send(at, way, corner_sum.at[:, part], back_corner.at[:, part])))
         at += 1
     back = {}
 
-    def pack_sides(start, size):
-        part = slice(start, start + size)
+    def pack_sides(begin, size):
+        part = slice(begin, begin + size)
         re, im = side_sum[0, part], side_sum[1, part]
         back_pack[0, part] = jnp.where(first_half, re, turned(im))
         back_pack[1, part] = jnp.where(first_half, turned(re), im)
 
-    def send_sides(start, size):
+    via_back = at
+    at += 6
+    numbers = {}
+
+    def send_sides(begin):
         nonlocal at
-        part = pl.ds(start, size)
+        part = pl.ds(begin, 64)
+        level = BACK_VIA.index(begin) if begin in BACK_VIA else None
         for slot, way in ((0, "right"), (1, "left")):
-            back[start, way] = send(at, way, back_pack.at[slot, part], back_got.at[slot, part])
+            numbers[begin, way] = at
+            target = back_got.at[slot, part]
+            back[begin, way] = send_chunk(at, way, back_pack.at[slot, part], target, back_hold.at[part], via_back, level)
             at += 1
 
     pack_sides(64, 128)
-    send_sides(64, 128)
+    send_sides(64)
+    send_sides(128)
     edge = []
-    for way, start in (("down", 0), ("up", 64)):
-        part = pl.ds(start, 64)
-        edge.append((way, start, send(at, way, ends_sum.at[:, part], back_ends.at[:, part])))
+    for way, begin in (("down", 0), ("up", 64)):
+        part = pl.ds(begin, 64)
+        edge.append((way, begin, send(at, way, ends_sum.at[:, part], back_ends.at[:, part])))
         at += 1
-    for way, start, made in grads:
+    for way, row, made in grads:
         receive(way, made)
-        begin = 0 if start == 0 else 192
-        side_sum[:, begin : begin + 64] = side_sum[:, begin : begin + 64] + back_corner[:, start : start + 64]
+        begin = 0 if row == 0 else 192
+        side_sum[:, begin : begin + 64] = side_sum[:, begin : begin + 64] + back_corner[:, row : row + 64]
         pack_sides(begin, 64)
-        send_sides(begin, 64)
-    for way, start, made in edge:
+        send_sides(begin)
+    for level, begin in enumerate(BACK_VIA):
+        part = pl.ds(begin, 64)
+        targets = {"left": back_got.at[1, part], "right": back_got.at[0, part]}
+        pass_chunk({way: numbers[begin, way] for way in targets}, targets, back_hold.at[part], via_back, level)
+    for way, row, made in edge:
         receive(way, made)
-        begin = 0 if start == 0 else 192
-        core_sum[:, begin : begin + 64] = core_sum[:, begin : begin + 64] + back_ends[:, start : start + 64]
+        begin = 0 if row == 0 else 192
+        core_sum[:, begin : begin + 64] = core_sum[:, begin : begin + 64] + back_ends[:, row : row + 64]
     out_ref[...] = core[...] - step_size * core_sum[...]
-    for start, size in ((64, 128), (0, 64), (192, 64)):
-        part = slice(start, start + size)
+    for begin in BACK_CHUNKS:
+        part = slice(begin, begin + 64)
         for way in ("right", "left"):
-            receive(way, back[start, way])
+            receive(way, back[begin, way])
         from_left, from_right = back_got[0, part], back_got[1, part]
         for at_part, left_part, right_part in (
             (0, from_left, turned(from_right)),
@@ -355,8 +459,8 @@
         ):
             out_ref[at_part, part, :HALF] = out_ref[at_part, part, :HALF] - step_size * jnp.where(first_half, left_part, 0.0)
             out_ref[at_part, part, HALF:] = out_ref[at_part, part, HALF:] - step_size * jnp.where(first_half, 0.0, right_part)
-    for way, made in sent:
-        @pl.when(has[way])
+    for condition, made in sent:
+        @pl.when(condition)
         def _():
             made.wait_send()
 
@@ -364,7 +468,7 @@
 def per_device(n_row, n_col, object_field, probe_field, intensity, view_offsets, view_counts):
     anywhere = pl.BlockSpec(memory_space=pl.ANY)
     vmem = pltpu.VMEM
-    n_copies = 20
+    n_copies = 32
     return pl.pallas_call(
         functools.partial(step_kernel, n_row, n_col),
         out_shape=jax.ShapeDtypeStruct(object_field.shape, f32),
@@ -379,10 +483,11 @@
             vmem((4, 2, 256, 256), f32), vmem((4, 2, 128, 256), f32),
             vmem((2, 256, 256), f32), vmem((2, 256, 128), f32), vmem((2, 128, 256), f32), vmem((2, 128, 128), f32),
             vmem((2, 256, 128), f32), vmem((2, 256, 128), f32), vmem((2, 128, 256), f32), vmem((2, 128, 128), f32),
+            vmem((64, 256), f32), vmem((256, 128), f32),
             pltpu.SemaphoreType.DMA((6,)), pltpu.SemaphoreType.DMA((n_copies,)), pltpu.SemaphoreType.DMA((n_copies,)),
         ],
         compiler_params=pltpu.CompilerParams(
-            collective_id=0, has_side_effects=True, vmem_limit_bytes=55574528
+            collective_id=0, has_side_effects=True, vmem_limit_bytes=53 * 2**20
         ),
     )(
         object_field, probe_field, intensity[0, 0], pltpu.with_memory_space_constraint(view_offsets[0, 0].T, pltpu.HBM), view_counts,

time: 43.6 us -> 42.9 us (0.984); the launches traced: 43.5 us -> 42.2 us
  Pallas kernels: 42.1 us -> 40.8 us
    pallas_call x1, Pallas kernels: 42.1 us -> 40.8 us  [per_device(): pl.pallas_call(functools.partial(step_kernel, n_row, n_col), out_shape=ja...]
where the time goes in v3:
time: 42.9 us; the launch traced here: 42.2 us
  Pallas kernels  40.8 us (95%)
  local copies, waits for them, and re-layouts  0.8 us (2%)
  between operations  0.66 us (2%)
    pallas_call x1, Pallas kernels, per_device(): pl.pallas_call(functools.partial(step_kernel, n_row, n_col), out_shape=ja...  40.8 us

profile of v3, /device:TPU:27, one launch (start us, length us, event | category | flops | bytes accessed | tf_op | source)
XLA Modules:
  0.0 42.2 jit_solution(16043317921525248464)
XLA Ops:
  0.7 40.8 %shard_map.64 = f32[2,256,256]{2,1,0:T(8,128)S(1)} custom-call(f32[2,256,256]{2,1,0:T(8,128)} %object_hbm.1, f32[2,256,256]{2,1,0:T(8,128)} %probe_hbm.1, f32[4,256,256]{2,1,0:T(8,128)} %bitcast.4, s32[2,4]{1,0:T(2,128)} %bitcast.5, s32[1,1]{1,0:T(1,128)S(6)} %copy.8.counts_hbm, bf16[10,256,256]{2,1,0:T(8,128)(2,1)} %constant.2.clone.tab_hbm), custom_call_target="tpu_custom_call" | custom-call | tf_op jit(solution)/shard_map/pallas_call | solution.py:472
  41.4 0.8 %copy.9 = f32[2,256,256]{2,1,0:T(8,128)} copy(f32[2,256,256]{2,1,0:T(8,128)S(1)} %shard_map.64) | data formatting | bytes 1048576

commit v4 on v3

--- a/solution.py
+++ b/solution.py
@@ -350,15 +350,15 @@
 
     at = 0
     fore = {}
+    ends_at = at
+    ends_begins = {"down": (192, 64), "up": (0, 0)}
+    send_ends(ends_at, core, ends, hold, ends_begins)
+    at += 6
     for begin, size in CHUNKS:
         for slot, way in ((0, "left"), (1, "right")):
             part = pl.ds(begin, size)
             fore[begin, way] = send(at, way, pack.at[slot, part], got.at[slot, part])
             at += 1
-    ends_at = at
-    ends_begins = {"down": (192, 64), "up": (0, 0)}
-    send_ends(ends_at, core, ends, hold, ends_begins)
-    at += 6
 
     for load in loads[1:]:
         load.wait()
@@ -367,10 +367,10 @@
     for number in range(4):
         prepare_intensity(measured, tab, scaled, number)
 
+    pass_ends(ends_at, ends, hold, ends_begins)
     for way in ("left", "right"):
         receive(way, fore[0, way])
     corner_up = send(at, "up", got.at[:, pl.ds(0, 64)], corner_got.at[:, pl.ds(0, 64)])
-    pass_ends(ends_at, ends, hold, ends_begins)
     for way in ("left", "right"):
         receive(way, fore[192, way])
     corner_down = send(at + 1, "down", got.at[:, pl.ds(192, 64)], corner_got.at[:, pl.ds(64, 64)])

time: 42.9 us -> 42.9 us (level)
  no operation moved by 1% of the time
where the time goes in v4:
time: 42.9 us; the launch traced here: 42.3 us
  Pallas kernels  40.8 us (95%)
  local copies, waits for them, and re-layouts  0.8 us (2%)
  between operations  0.66 us (2%)
    pallas_call x1, Pallas kernels, per_device(): pl.pallas_call(functools.partial(step_kernel, n_row, n_col), out_shape=ja...  40.8 us

profile of v4, /device:TPU:27, one launch (start us, length us, event | category | flops | bytes accessed | tf_op | source)
XLA Modules:
  0.0 42.3 jit_solution(7227691476132564468)
XLA Ops:
  0.7 40.8 %shard_map.64 = f32[2,256,256]{2,1,0:T(8,128)S(1)} custom-call(f32[2,256,256]{2,1,0:T(8,128)} %object_hbm.1, f32[2,256,256]{2,1,0:T(8,128)} %probe_hbm.1, f32[4,256,256]{2,1,0:T(8,128)} %bitcast.4, s32[2,4]{1,0:T(2,128)} %bitcast.5, s32[1,1]{1,0:T(1,128)S(6)} %copy.8.counts_hbm, bf16[10,256,256]{2,1,0:T(8,128)(2,1)} %constant.2.clone.tab_hbm), custom_call_target="tpu_custom_call" | custom-call | tf_op jit(solution)/shard_map/pallas_call | solution.py:472
  41.5 0.8 %copy.9 = f32[2,256,256]{2,1,0:T(8,128)} copy(f32[2,256,256]{2,1,0:T(8,128)S(1)} %shard_map.64) | data formatting | bytes 1048576
